TPU v7x, 32 devices: a whole 2x2x4 slice. The times are simulated.
32 devices in a mesh: section: 4 (over y, x), expert: 8 (over z, core).
Axes of the slice: x: 2, y: 2, z: 4, core: 2. Of those that a mesh axis runs over, the one named last changes fastest.
Arguments:
- forward_input: bfloat16 [4, 576, 4096], P('section', 'expert'), may hold values from -6 to 6
- backward_cotangent: bfloat16 [4, 576, 4096], P('section', 'expert'), may hold values from -6 to 6
- saved_input: bfloat16 [4, 576, 4096], P('section', 'expert'), may hold values from -6 to 6
- saved_hidden: bfloat16 [4, 8, 360, 1536], P('section', 'expert'), may hold values from -8 to 8
- norm_gain: float32 [4, 4096], P('section'), may hold values from 0.5 to 2
- forward_experts: int32 [4, 576, 4], P('section', 'expert'), may hold values from 0 to 7, all different within a row; in each aligned block of 72 rows (0 to 71, 72 to 143, ..., all dimensions but the last counted through in order) at most 45 rows name the same one
- forward_gates: float32 [4, 576, 4], P('section', 'expert'), may hold values from 0.05 to 1
- backward_experts: int32 [4, 576, 4], P('section', 'expert'), may hold values from 0 to 7, all different within a row; in each aligned block of 72 rows (0 to 71, 72 to 143, ..., all dimensions but the last counted through in order) at most 45 rows name the same one
- backward_gates: float32 [4, 576, 4], P('section', 'expert'), may hold values from 0.05 to 1
- gate_up_weight: bfloat16 [4, 8, 4096, 1536], P('section', 'expert'), may hold values from -0.09375 to 0.09375
- down_weight: bfloat16 [4, 8, 768, 4096], P('section', 'expert'), may hold values from -0.21875 to 0.21875
Outputs:
- forward_output: bfloat16 [4, 576, 4096], P('section', 'expert')
- input_gradient: bfloat16 [4, 576, 4096], P('section', 'expert')
Inputs may be any that keep to these rules, and one draw needn't show every extreme that they name: `forward_experts`: each token names 4 distinct experts. In the rows of one device (aligned blocks of 72 tokens) no expert is named by more than 45 entries, and in some device's rows some expert is named by exactly 45. `backward_experts`: same law as forward_experts, drawn independently.
All inputs are finite; a program needn't handle non-finite values.
Results may differ from a plain program's by a relative error of at most 0.0054.
Values may be sent and summed in bfloat16 or wider, within the bound.
A program may use at most 128 MiB of HBM per device.

v0:
```python
import jax
import jax.numpy as jnp
from jax import lax
from jax.sharding import PartitionSpec as P

EPSILON = 1e-06


def passed_along(value, axis, steps):
    count = lax.axis_size(axis)
    initial, last = (max(0, -steps), min(count, count - steps))
    return lax.ppermute(value, axis, [(source, source + steps) for source in range(initial, last)])


def norm_scale(values, gain_row):
    widened = values.astype(jnp.float32)
    inverse = lax.rsqrt(jnp.mean(widened * widened, axis=-1, keepdims=True) + EPSILON)
    return widened * inverse * gain_row


def dense_weights(expert_ids, gates, expert_count):
    weights = gates / jnp.sum(gates, axis=-1, keepdims=True)
    onehot = expert_ids[:, :, None] == jnp.arange(expert_count, dtype=jnp.int32)[None, None, :]
    return jnp.sum(jnp.where(onehot, weights[:, :, None], 0.0), axis=1)


def local(
    forward_input,
    backward_cotangent,
    saved_input,
    saved_hidden,
    norm_gain,
    forward_experts,
    forward_gates,
    backward_experts,
    backward_gates,
    gate_up_weight,
    down_weight,
):
    peer_count = lax.axis_size("expert")
    me = lax.axis_index("expert")
    table = jnp.concatenate(
        [
            dense_weights(forward_experts[0], forward_gates[0], peer_count),
            dense_weights(backward_experts[0], backward_gates[0], peer_count),
        ],
        axis=1,
    )
    tables = lax.all_gather(table, "expert", axis=0, tiled=True)
    weight_f = lax.dynamic_slice_in_dim(tables, me, 1, axis=1)
    weight_b = lax.dynamic_slice_in_dim(tables, peer_count + me, 1, axis=1)
    moved_input, moved_cotangent = passed_along((forward_input, backward_cotangent), "section", 1)
    is_first = lax.axis_index("section") == 0
    layer_in = jnp.where(is_first, forward_input, moved_input)[0]
    cotangent = jnp.where(is_first, backward_cotangent, moved_cotangent)[0]
    token_count = layer_in.shape[0]
    slot_total = saved_hidden.shape[2]
    capacity = slot_total // peer_count
    gain_row = norm_gain[0]
    weight_in = gate_up_weight[0, 0]
    weight_down = down_weight[0, 0]
    hidden_width = weight_down.shape[0]
    normed = norm_scale(layer_in, gain_row).astype(jnp.bfloat16)
    all_normed = lax.all_gather(normed, "expert", axis=0, tiled=True)
    all_cotangent = lax.all_gather(cotangent, "expert", axis=0, tiled=True)
    projected = jnp.dot(all_normed, weight_in, preferred_element_type=jnp.float32)
    hidden = (jax.nn.silu(projected[:, :hidden_width]) * projected[:, hidden_width:]).astype(
        jnp.bfloat16
    )
    served = jnp.dot(hidden, weight_down, preferred_element_type=jnp.float32)
    served = (served * weight_f).astype(jnp.bfloat16)
    mixture = lax.psum_scatter(served, "expert", scatter_dimension=0, tiled=True)
    forward_output = (layer_in.astype(jnp.float32) + mixture.astype(jnp.float32)).astype(
        jnp.bfloat16
    )
    routed = (weight_b > 0.0).reshape(peer_count, token_count)
    slot = jnp.cumsum(routed.astype(jnp.int32), axis=1) - 1
    spread = (
        (slot[:, :, None] == jnp.arange(capacity, dtype=jnp.int32)[None, None, :])
        & routed[:, :, None]
    ).astype(jnp.bfloat16)
    saved = jnp.einsum(
        "jts,jsf->jtf",
        spread,
        saved_hidden[0, 0].reshape(peer_count, capacity, -1),
        preferred_element_type=jnp.float32,
    ).reshape(peer_count * token_count, -1)
    scaled = (weight_b * all_cotangent.astype(jnp.float32)).astype(jnp.bfloat16)
    grad_hidden = lax.dot_general(
        scaled, weight_down, (((1,), (1,)), ((), ())), preferred_element_type=jnp.float32
    )
    gate, up = (saved[:, :hidden_width], saved[:, hidden_width:])
    sig = jax.nn.sigmoid(gate)
    grad_both = jnp.concatenate(
        [grad_hidden * up * sig * (1.0 + gate * (1.0 - sig)), grad_hidden * gate * sig], axis=1
    ).astype(jnp.bfloat16)
    grads = lax.dot_general(
        grad_both, weight_in, (((1,), (1,)), ((), ())), preferred_element_type=jnp.float32
    ).astype(jnp.bfloat16)
    grad_normed = lax.psum_scatter(grads, "expert", scatter_dimension=0, tiled=True).astype(
        jnp.float32
    )

    def apply_norm(inputs):
        return norm_scale(inputs, gain_row)

    primal, pullback = jax.vjp(apply_norm, saved_input[0].astype(jnp.float32))
    input_gradient = (cotangent.astype(jnp.float32) + pullback(grad_normed)[0]).astype(jnp.bfloat16)
    return (forward_output[None], input_gradient[None])


def solution(mesh):
    row = P("section", "expert", None)
    block = P("section", "expert", None, None)
    in_specs = (row, row, row, block, P("section", None), row, row, row, row, block, block)
    return jax.shard_map(local, mesh=mesh, in_specs=in_specs, out_specs=(row, row), check_vma=False)
```

profile of v0, /device:TPU:0, one launch (start us, length us, event | category | flops | bytes accessed | tf_op | source)
XLA Modules:
  0.0 298.4 jit_solution(10791374151857974960)
XLA Ops:
  7.2 0.0 copy-start.5
  7.2 0.0 copy-start.6
  7.2 0.0 copy-start.7
  7.2 0.0 copy-start.8
  7.2 0.0 copy-start.2
  7.2 0.0 all-gather.7.cloned.1.call-start
  7.3 5.0 %collective-permute-start.1 = (bf16[1,72,4096]{2,1,0:T(8,128)(2,1)}, bf16[1,72,4096]{2,1,0:T(8,128)(2,1)S(1)}, u32[]{:S(2)}, u32[]{:S(2)}) collective-permute-start(bf16[1,72,4096]{2,1,0:T(8,128)(2,1)} %param.12), channel_id=1, source_target_pairs={{0,8},{8,16},{16,24},{1,9},{9,17},{17,25},{2,10},{10,18},{18,26},{... | collective-permute-start | bytes 1769480 | tf_op jit(solution)/shard_map/ppermute | solution.py:12
  12.3 12.8 %collective-permute-done.1 = bf16[1,72,4096]{2,1,0:T(8,128)(2,1)S(1)} collective-permute-done((bf16[1,72,4096]{2,1,0:T(8,128)(2,1)}, bf16[1,72,4096]{2,1,0:T(8,128)(2,1)S(1)}, u32[]{:S(2)}, u32[]{:S(2)}) %collective-permute-start.1) | collective-permute-done | bytes 589856 | tf_op jit(solution)/shard_map/ppermute | solution.py:12
  25.1 2.0 broadcast_select_fusion
  27.1 0.0 all-gather.7.cloned.1.call-update
  27.1 0.0 reduce-scatter.5.cloned.1.call-start
  27.2 0.0 copy-done.5
  27.2 0.0 copy-done.6
  27.2 0.0 copy-done.7
  27.3 0.0 copy-done.8
  27.3 14.3 %all-gather.1 = f32[8,72,16]{1,2,0:T(8,128)S(1)} all-gather(f32[1,72,16]{1,2,0:T(8,128)S(1)} %maximum_bitcast_fusion), channel_id=1, replica_groups=mesh['section'=4,'expert'=8] {'expert'}, dimensions={0}, use_global_device_ids=true | all-gather | bytes 41472 | tf_op jit(solution)/shard_map/all_gather | solution.py:49
  41.6 0.1 reshape.100
  41.7 0.0 copy-done.2
  41.7 0.3 reshape_squeeze.3
  42.1 0.1 reshape.92
  42.2 0.2 reduce_window_sum.11
  42.5 2.4 fusion.34
  44.9 35.2 %all-gather.7.cloned.1.call-done = bf16[1,576,4096]{2,1,0:T(8,128)(2,1)} async-done(((bf16[1,72,4096]{2,1,0:T(8,128)(2,1)}), bf16[1,576,4096]{2,1,0:T(8,128)(2,1)}) %all-gather.7.cloned.1.call-update) | async-done | bytes 4718608 | tf_op jit(solution)/shard_map/all_gather | solution.py:65
  80.1 9.4 %fusion.16 = (bf16[576,768]{1,0:T(8,128)(2,1)S(1)}, bf16[576,768]{1,0:T(8,128)(2,1)S(1)}) fusion(f32[576,1536]{1,0:T(8,128)} %bitcast.55, bf16[1,1,768,4096]{3,2,1,0:T(8,128)(2,1)} %param.21, bf16[1,576,4096]{2,1,0:T(8,128)(2,1)} %all-gather.7.cloned.1.call-done, f32[576]{0:T(1024)S(1)} %get-tuple-element.4), kind=kOutput, calls=%fused_computation.16 | convolution fusion | flops 3636707328 | bytes 16320768 | tf_op jit(solution)/shard_map/dot_general | solution.py:89
  89.6 18.4 %fusion.8 = bf16[576,4096]{1,0:T(8,128)(2,1)} fusion(bf16[1,1,4096,1536]{3,2,1,0:T(8,128)(2,1)} %param.20, bf16[576,768]{1,0:T(8,128)(2,1)S(1)} %get-tuple-element.9, bf16[576,768]{1,0:T(8,128)(2,1)S(1)} %get-tuple-element.8), kind=kOutput, calls=%fused_computation.10 | convolution fusion | flops 7253655552 | bytes 19070976 | tf_op jit(solution)/shard_map/dot_general | solution.py:97
  107.9 0.0 copy-start.3
  107.9 0.0 reduce-scatter.5.cloned.1.call-update
  107.9 0.0 copy-start.1
  107.9 0.0 copy-start.4
  108.0 0.0 copy-start
  108.0 0.0 all-gather.5.cloned.1.call-start
  108.0 1.0 copy-done.3
  109.0 3.4 %collective-permute-start = (bf16[1,72,4096]{2,1,0:T(8,128)(2,1)S(1)}, bf16[1,72,4096]{2,1,0:T(8,128)(2,1)S(1)}, u32[]{:S(2)}, u32[]{:S(2)}) collective-permute-start(bf16[1,72,4096]{2,1,0:T(8,128)(2,1)S(1)} %copy-done.3), channel_id=1, source_target_pairs={{0,8},{8,16},{16,24},{1,9},{9,17},{17,25},{2,10},{10,18},{18,26},{... | collective-permute-start | bytes 1769480 | tf_op jit(solution)/shard_map/ppermute | solution.py:12
  112.4 12.9 %collective-permute-done = bf16[1,72,4096]{2,1,0:T(8,128)(2,1)S(1)} collective-permute-done((bf16[1,72,4096]{2,1,0:T(8,128)(2,1)S(1)}, bf16[1,72,4096]{2,1,0:T(8,128)(2,1)S(1)}, u32[]{:S(2)}, u32[]{:S(2)}) %collective-permute-start) | collective-permute-done | bytes 589856 | tf_op jit(solution)/shard_map/ppermute | solution.py:12
  125.3 0.3 fusion.23
  125.6 36.1 %reduce-scatter.5.cloned.1.call-done = bf16[72,4096]{1,0:T(8,128)(2,1)} async-done(((bf16[576,4096]{1,0:T(8,128)(2,1)}), bf16[72,4096]{1,0:T(8,128)(2,1)}) %reduce-scatter.5.cloned.1.call-update) | async-done | bytes 589840 | tf_op jit(solution)/shard_map/reduce_scatter | solution.py:100
  161.7 0.0 copy-done.1
  161.7 0.0 copy-done.4
  161.7 1.4 fusion.27
  163.2 0.0 copy-done
  163.2 2.6 fusion.32
  165.9 0.0 all-gather.5.cloned.1.call-update
  165.9 0.2 reduce-scatter.3.cloned.1.call-start
  166.1 50.0 %all-gather.5.cloned.1.call-done = bf16[576,4096]{1,0:T(8,128)(2,1)} async-done(((bf16[72,4096]{1,0:T(8,128)(2,1)}), bf16[576,4096]{1,0:T(8,128)(2,1)}) %all-gather.5.cloned.1.call-update) | async-done | bytes 4718608 | tf_op jit(solution)/shard_map/all_gather | solution.py:64
  216.1 11.5 %fusion.2 = f32[576,1536]{1,0:T(8,128)S(1)} fusion(bf16[576,4096]{1,0:T(8,128)(2,1)} %all-gather.5.cloned.1.call-done, bf16[1,1,4096,1536]{3,2,1,0:T(8,128)(2,1)} %param.20), kind=kOutput, calls=%fused_computation.2 | convolution fusion | flops 7247757312 | bytes 20840448 | tf_op jit(solution)/shard_map/dot_general | solution.py:66
  227.5 8.4 %multiply_convert_fusion = bf16[576,4096]{1,0:T(8,128)(2,1)} fusion(bf16[1,1,768,4096]{3,2,1,0:T(8,128)(2,1)} %param.21, f32[576]{0:T(1024)S(1)} %get-tuple-element.5, f32[576,1536]{1,0:T(8,128)S(1)} %fusion.2), kind=kOutput, calls=%fused_computation.6 | convolution fusion | flops 3631251456 | bytes 14551296 | tf_op jit(solution)/shard_map/dot_general | solution.py:70
  235.9 0.0 reduce-scatter.3.cloned.1.call-update
  235.9 53.9 %reduce-scatter.3.cloned.1.call-done = bf16[72,4096]{1,0:T(8,128)(2,1)} async-done(((bf16[576,4096]{1,0:T(8,128)(2,1)}), bf16[72,4096]{1,0:T(8,128)(2,1)}) %reduce-scatter.3.cloned.1.call-update) | async-done | bytes 589840 | tf_op jit(solution)/shard_map/reduce_scatter | solution.py:72
  289.9 2.0 fusion.31
  (13 shorter events, 0.2 us)
Async XLA Ops:
  7.2 20.0 %copy-start.5 = (f32[1,72,4]{1,2,0:T(4,128)S(1)}, f32[1,72,4]{1,2,0:T(4,128)}, u32[]{:S(2)}) copy-start(f32[1,72,4]{1,2,0:T(4,128)} %param.19) | copy-start | bytes 3460
  7.2 20.0 %copy-start.6 = (f32[1,72,4]{1,2,0:T(4,128)S(1)}, f32[1,72,4]{1,2,0:T(4,128)}, u32[]{:S(2)}) copy-start(f32[1,72,4]{1,2,0:T(4,128)} %param.17) | copy-start | bytes 3460
  7.2 20.1 %copy-start.7 = (s32[1,72,4]{1,2,0:T(4,128)S(1)}, s32[1,72,4]{1,2,0:T(4,128)}, u32[]{:S(2)}) copy-start(s32[1,72,4]{1,2,0:T(4,128)} %param.18) | copy-start | bytes 3460
  7.2 20.1 %copy-start.8 = (s32[1,72,4]{1,2,0:T(4,128)S(1)}, s32[1,72,4]{1,2,0:T(4,128)}, u32[]{:S(2)}) copy-start(s32[1,72,4]{1,2,0:T(4,128)} %param.16) | copy-start | bytes 3460
  7.2 34.5 %copy-start.2 = (bf16[1,1,360,1536]{3,2,1,0:T(8,128)(2,1)S(1)}, bf16[1,1,360,1536]{3,2,1,0:T(8,128)(2,1)}, u32[]{:S(2)}) copy-start(bf16[1,1,360,1536]{3,2,1,0:T(8,128)(2,1)} %param.14) | copy-start | bytes 3317764
  7.2 72.9 %all-gather.7.cloned.1.call-start = ((), (), s32[]{:S(2)}) async-start(), calls=%async_computation.5 | async-start | bytes 5308416 | tf_op jit(solution)/shard_map/all_gather | solution.py:65
  7.3 17.9 %collective-permute-start.1 = (bf16[1,72,4096]{2,1,0:T(8,128)(2,1)}, bf16[1,72,4096]{2,1,0:T(8,128)(2,1)S(1)}, u32[]{:S(2)}, u32[]{:S(2)}) collective-permute-start(bf16[1,72,4096]{2,1,0:T(8,128)(2,1)} %param.12), channel_id=1, source_target_pairs={{0,8},{8,16},{16,24},{1,9},{9,17},{17,25},{2,10},{10,18},{18,26},{... | collective-permute-start | bytes 1769480 | tf_op jit(solution)/shard_map/ppermute | solution.py:12
  27.1 134.6 %reduce-scatter.5.cloned.1.call-start = ((), (), s32[]{:S(2)}) async-start(), calls=%async_computation.4 | async-start | bytes 5308416 | tf_op jit(solution)/shard_map/reduce_scatter | solution.py:100
  107.9 1.1 copy-start.3
  107.9 53.8 %copy-start.1 = (bf16[1,72,4096]{2,1,0:T(8,128)(2,1)S(1)}, bf16[1,72,4096]{2,1,0:T(8,128)(2,1)}, u32[]{:S(2)}) copy-start(bf16[1,72,4096]{2,1,0:T(8,128)(2,1)} %param.13) | copy-start | bytes 1769476
  107.9 53.8 %copy-start.4 = (f32[1,4096]{1,0:T(1,128)S(1)}, f32[1,4096]{1,0:T(1,128)}, u32[]{:S(2)}) copy-start(f32[1,4096]{1,0:T(1,128)} %param.15) | copy-start | bytes 49156
  108.0 55.2 %copy-start = (bf16[1,72,4096]{2,1,0:T(8,128)(2,1)S(1)}, bf16[1,72,4096]{2,1,0:T(8,128)(2,1)}, u32[]{:S(2)}) copy-start(bf16[1,72,4096]{2,1,0:T(8,128)(2,1)} %broadcast_select_fusion) | copy-start | bytes 1769476
  108.0 108.1 %all-gather.5.cloned.1.call-start = ((), (), s32[]{:S(2)}) async-start(), calls=%async_computation.2 | async-start | bytes 5308416 | tf_op jit(solution)/shard_map/all_gather | solution.py:64
  109.0 16.3 %collective-permute-start = (bf16[1,72,4096]{2,1,0:T(8,128)(2,1)S(1)}, bf16[1,72,4096]{2,1,0:T(8,128)(2,1)S(1)}, u32[]{:S(2)}, u32[]{:S(2)}) collective-permute-start(bf16[1,72,4096]{2,1,0:T(8,128)(2,1)S(1)} %copy-done.3), channel_id=1, source_target_pairs={{0,8},{8,16},{16,24},{1,9},{9,17},{17,25},{2,10},{10,18},{18,26},{... | collective-permute-start | bytes 1769480 | tf_op jit(solution)/shard_map/ppermute | solution.py:12
  165.9 124.0 %reduce-scatter.3.cloned.1.call-start = ((), (), s32[]{:S(2)}) async-start(), calls=%async_computation.3 | async-start | bytes 5308416 | tf_op jit(solution)/shard_map/reduce_scatter | solution.py:72
Sparse Core Ops, SparseCore 0:
  27.2 52.8 all-gather.6
  108.1 53.6 reduce-scatter.4
  166.0 50.0 all-gather.4
  236.1 53.7 reduce-scatter.2
where the time goes:
time: 299 us; the launch traced here: 298 us
  waiting for transfers between devices  201 us (67%)
  matrix products  50 us (17%)
  blocking collectives  14.3 us (5%)
  between operations  14 us (5%)
  starting transfers between devices  8.75 us (3%)
  other arithmetic  8.72 us (3%)
    reduce_scatter x1, waiting for transfers between devices, local(): lax.psum_scatter(served, 'expert', scatter_dimension=0, tiled=True)  53.9 us
    all_gather x1, waiting for transfers between devices, local(): all_normed = lax.all_gather(normed, 'expert', axis=0, tiled=True)  50 us
    reduce_scatter x1, waiting for transfers between devices, local(): lax.psum_scatter(grads, 'expert', scatter_dimension=0, tiled=True)  36.1 us
    all_gather x1, waiting for transfers between devices, local(): all_cotangent = lax.all_gather(cotangent, 'expert', axis=0, tiled=True)  35.2 us
    ppermute x2, waiting for transfers between devices, passed_along(): lax.ppermute(value, axis, [(source, source + steps) for source in range(i...  25.8 us
    dot_general x1, matrix products, local(): lax.dot_general(grad_both, weight_in, (((1,), (1,)), ((), ())), preferred...  18.4 us
    all_gather x1, blocking collectives, local(): tables = lax.all_gather(table, 'expert', axis=0, tiled=True)  14.3 us
    dot_general x1, matrix products, local(): jnp.dot(all_normed, weight_in, preferred_element_type=jnp.float32)  11.5 us
  transfers between devices with their start and end apart: 6, of which 6 were waited for; matrix products, arithmetic and copies ran while one was open for 1% of the time, Pallas kernels for 0%

commit v1 on v0

--- a/solution.py
+++ b/solution.py
@@ -4,6 +4,16 @@
 from jax.sharding import PartitionSpec as P
 
 EPSILON = 1e-06
+
+
+def around_the_ring(x, axis, d):
+    n_dev = lax.axis_size(axis)
+    held, pieces = (x, [x])
+    for _ in range(n_dev - 1):
+        held = lax.ppermute(held, axis, [(i, (i + 1) % n_dev) for i in range(n_dev)])
+        pieces.insert(0, held)
+    line = jnp.concatenate(pieces, axis=d)
+    return jnp.roll(line, (lax.axis_index(axis) + 1) * x.shape[d], axis=d)
 
 
 def passed_along(value, axis, steps):
@@ -46,7 +56,7 @@
         ],
         axis=1,
     )
-    tables = lax.all_gather(table, "expert", axis=0, tiled=True)
+    tables = around_the_ring(table, "expert", 0)
     weight_f = lax.dynamic_slice_in_dim(tables, me, 1, axis=1)
     weight_b = lax.dynamic_slice_in_dim(tables, peer_count + me, 1, axis=1)
     moved_input, moved_cotangent = passed_along((forward_input, backward_cotangent), "section", 1)

time: 299 us -> 299 us (level)
  waiting for transfers between devices: 201 us -> 216 us
  blocking collectives: 14.3 us -> 0 us
    ppermute x0 -> x7, waiting for transfers between devices: none -> 34.7 us  [around_the_ring(): lax.ppermute(held, axis, [(i, (i + 1) % n_dev) for i in range(n_dev)])]
    all_gather x1, waiting for transfers between devices: 35.2 us -> 14.9 us  [local(): all_cotangent = lax.all_gather(cotangent, 'expert', axis=0, tiled=True)]
    all_gather x1 -> x0, blocking collectives: 14.3 us -> none  [local(): tables = lax.all_gather(table, 'expert', axis=0, tiled=True)]
  transfers between devices with their start and end apart: 6 -> 13, of which waited for: 6 -> 13; matrix products, arithmetic and copies ran while one was open for 1% -> 1% of each run, Pallas kernels for 0% -> 0%
where the time goes in v1:
time: 299 us
  waiting for transfers between devices  216 us (72%)
  matrix products  50 us (17%)
  between operations  14 us (5%)
  starting transfers between devices  8.79 us (3%)
  other arithmetic  8.79 us (3%)
    reduce_scatter x1, waiting for transfers between devices, local(): lax.psum_scatter(served, 'expert', scatter_dimension=0, tiled=True)  53.9 us
    all_gather x1, waiting for transfers between devices, local(): all_normed = lax.all_gather(normed, 'expert', axis=0, tiled=True)  50 us
    reduce_scatter x1, waiting for transfers between devices, local(): lax.psum_scatter(grads, 'expert', scatter_dimension=0, tiled=True)  36.3 us
    ppermute x7, waiting for transfers between devices, around_the_ring(): lax.ppermute(held, axis, [(i, (i + 1) % n_dev) for i in range(n_dev)])  34.7 us
    ppermute x2, waiting for transfers between devices, passed_along(): lax.ppermute(value, axis, [(source, source + steps) for source in range(i...  25.8 us
    dot_general x1, matrix products, local(): lax.dot_general(grad_both, weight_in, (((1,), (1,)), ((), ())), preferred...  18.4 us
    all_gather x1, waiting for transfers between devices, local(): all_cotangent = lax.all_gather(cotangent, 'expert', axis=0, tiled=True)  14.9 us
    dot_general x1, matrix products, local(): jnp.dot(all_normed, weight_in, preferred_element_type=jnp.float32)  11.5 us
  transfers between devices with their start and end apart: 13, of which 13 were waited for; matrix products, arithmetic and copies ran while one was open for 1% of the time, Pallas kernels for 0%

profile of v1, /device:TPU:0, one launch (start us, length us, event | category | flops | bytes accessed | tf_op | source)
XLA Modules:
  0.0 298.8 jit_solution(8016240804026072334)
XLA Ops:
  7.2 0.0 copy-start.5
  7.2 0.0 copy-start.6
  7.2 0.0 copy-start.7
  7.2 0.0 copy-start.8
  7.2 0.0 copy-start.2
  7.2 0.0 all-gather.6.cloned.1.call-start
  7.3 5.0 %collective-permute-start.8 = (bf16[1,72,4096]{2,1,0:T(8,128)(2,1)}, bf16[1,72,4096]{2,1,0:T(8,128)(2,1)S(1)}, u32[]{:S(2)}, u32[]{:S(2)}) collective-permute-start(bf16[1,72,4096]{2,1,0:T(8,128)(2,1)} %param.12), channel_id=1, source_target_pairs={{0,8},{8,16},{16,24},{1,9},{9,17},{17,25},{2,10},{10,18},{18,26},{... | collective-permute-start | bytes 1769480 | tf_op jit(solution)/shard_map/ppermute | solution.py:22
  12.3 12.8 %collective-permute-done.8 = bf16[1,72,4096]{2,1,0:T(8,128)(2,1)S(1)} collective-permute-done((bf16[1,72,4096]{2,1,0:T(8,128)(2,1)}, bf16[1,72,4096]{2,1,0:T(8,128)(2,1)S(1)}, u32[]{:S(2)}, u32[]{:S(2)}) %collective-permute-start.8) | collective-permute-done | bytes 589856 | tf_op jit(solution)/shard_map/ppermute | solution.py:22
  25.1 2.0 broadcast_select_fusion
  27.1 0.0 all-gather.6.cloned.1.call-update
  27.1 0.0 reduce-scatter.5.cloned.1.call-start
  27.2 0.0 copy-done.5
  27.2 0.0 copy-done.6
  27.2 0.0 copy-done.7
  27.2 0.0 copy-done.8
  27.3 0.1 collective-permute-start.1
  27.4 4.9 %collective-permute-done.1 = f32[72,16]{0,1:T(8,128)S(1)} collective-permute-done((f32[72,16]{0,1:T(8,128)S(1)}, f32[72,16]{0,1:T(8,128)S(1)}, u32[]{:S(2)}, u32[]{:S(2)}) %collective-permute-start.1) | collective-permute-done | bytes 4640 | tf_op jit(solution)/shard_map/ppermute | solution.py:13
  32.2 0.0 collective-permute-start.2
  32.2 4.9 %collective-permute-done.2 = f32[72,16]{0,1:T(8,128)S(1)} collective-permute-done((f32[72,16]{0,1:T(8,128)S(1)}, f32[72,16]{0,1:T(8,128)S(1)}, u32[]{:S(2)}, u32[]{:S(2)}) %collective-permute-start.2) | collective-permute-done | bytes 4640 | tf_op jit(solution)/shard_map/ppermute | solution.py:13
  37.1 0.0 collective-permute-start.3
  37.1 5.0 %collective-permute-done.3 = f32[72,16]{0,1:T(8,128)S(1)} collective-permute-done((f32[72,16]{0,1:T(8,128)S(1)}, f32[72,16]{0,1:T(8,128)S(1)}, u32[]{:S(2)}, u32[]{:S(2)}) %collective-permute-start.3) | collective-permute-done | bytes 4640 | tf_op jit(solution)/shard_map/ppermute | solution.py:13
  42.1 0.0 collective-permute-start.4
  42.1 5.0 %collective-permute-done.4 = f32[72,16]{0,1:T(8,128)S(1)} collective-permute-done((f32[72,16]{0,1:T(8,128)S(1)}, f32[72,16]{0,1:T(8,128)S(1)}, u32[]{:S(2)}, u32[]{:S(2)}) %collective-permute-start.4) | collective-permute-done | bytes 4640 | tf_op jit(solution)/shard_map/ppermute | solution.py:13
  47.2 0.0 collective-permute-start.5
  47.2 5.0 %collective-permute-done.5 = f32[72,16]{0,1:T(8,128)S(1)} collective-permute-done((f32[72,16]{0,1:T(8,128)S(1)}, f32[72,16]{0,1:T(8,128)S(1)}, u32[]{:S(2)}, u32[]{:S(2)}) %collective-permute-start.5) | collective-permute-done | bytes 4640 | tf_op jit(solution)/shard_map/ppermute | solution.py:13
  52.2 0.0 collective-permute-start.6
  52.2 5.1 %collective-permute-done.6 = f32[72,16]{0,1:T(8,128)S(1)} collective-permute-done((f32[72,16]{0,1:T(8,128)S(1)}, f32[72,16]{0,1:T(8,128)S(1)}, u32[]{:S(2)}, u32[]{:S(2)}) %collective-permute-start.6) | collective-permute-done | bytes 4640 | tf_op jit(solution)/shard_map/ppermute | solution.py:13
  57.3 0.0 collective-permute-start.7
  57.3 0.0 copy-done.2
  57.3 0.3 reshape_squeeze.3
  57.6 4.8 %collective-permute-done.7 = f32[72,16]{0,1:T(8,128)S(1)} collective-permute-done((f32[72,16]{0,1:T(8,128)S(1)}, f32[72,16]{0,1:T(8,128)S(1)}, u32[]{:S(2)}, u32[]{:S(2)}) %collective-permute-start.7) | collective-permute-done | bytes 4640 | tf_op jit(solution)/shard_map/ppermute | solution.py:13
  62.4 0.1 concatenate.14
  62.5 0.1 compare_reduce_fusion
  62.6 0.1 reshape.92
  62.7 0.2 reduce_window_sum.11
  62.9 0.1 dynamic-slice_reduce_fusion.1
  63.1 2.4 fusion.39
  65.5 14.9 %all-gather.6.cloned.1.call-done = bf16[1,576,4096]{2,1,0:T(8,128)(2,1)} async-done(((bf16[1,72,4096]{2,1,0:T(8,128)(2,1)}), bf16[1,576,4096]{2,1,0:T(8,128)(2,1)}) %all-gather.6.cloned.1.call-update) | async-done | bytes 4718608 | tf_op jit(solution)/shard_map/all_gather | solution.py:75
  80.4 9.4 %fusion.17 = (bf16[576,768]{1,0:T(8,128)(2,1)S(1)}, bf16[576,768]{1,0:T(8,128)(2,1)S(1)}) fusion(f32[576,1536]{1,0:T(8,128)} %bitcast.53, bf16[1,1,768,4096]{3,2,1,0:T(8,128)(2,1)} %param.21, bf16[1,576,4096]{2,1,0:T(8,128)(2,1)} %all-gather.6.cloned.1.call-done, f32[576]{0:T(1024)S(1)} %get-tuple-element.4), kind=kOutput, calls=%fused_computation.17 | convolution fusion | flops 3636707328 | bytes 16320768 | tf_op jit(solution)/shard_map/dot_general | solution.py:99
  89.8 18.4 %fusion.9 = bf16[576,4096]{1,0:T(8,128)(2,1)} fusion(bf16[1,1,4096,1536]{3,2,1,0:T(8,128)(2,1)} %param.20, bf16[576,768]{1,0:T(8,128)(2,1)S(1)} %get-tuple-element.9, bf16[576,768]{1,0:T(8,128)(2,1)S(1)} %get-tuple-element.8), kind=kOutput, calls=%fused_computation.11 | convolution fusion | flops 7253655552 | bytes 19070976 | tf_op jit(solution)/shard_map/dot_general | solution.py:107
  108.2 0.0 copy-start.3
  108.2 0.0 reduce-scatter.5.cloned.1.call-update
  108.2 0.0 copy-start.1
  108.2 0.0 copy-start.4
  108.2 0.0 copy-start
  108.2 0.0 all-gather.4.cloned.1.call-start
  108.3 1.0 copy-done.3
  109.2 3.4 %collective-permute-start = (bf16[1,72,4096]{2,1,0:T(8,128)(2,1)S(1)}, bf16[1,72,4096]{2,1,0:T(8,128)(2,1)S(1)}, u32[]{:S(2)}, u32[]{:S(2)}) collective-permute-start(bf16[1,72,4096]{2,1,0:T(8,128)(2,1)S(1)} %copy-done.3), channel_id=1, source_target_pairs={{0,8},{8,16},{16,24},{1,9},{9,17},{17,25},{2,10},{10,18},{18,26},{... | collective-permute-start | bytes 1769480 | tf_op jit(solution)/shard_map/ppermute | solution.py:22
  112.6 12.9 %collective-permute-done = bf16[1,72,4096]{2,1,0:T(8,128)(2,1)S(1)} collective-permute-done((bf16[1,72,4096]{2,1,0:T(8,128)(2,1)S(1)}, bf16[1,72,4096]{2,1,0:T(8,128)(2,1)S(1)}, u32[]{:S(2)}, u32[]{:S(2)}) %collective-permute-start) | collective-permute-done | bytes 589856 | tf_op jit(solution)/shard_map/ppermute | solution.py:22
  125.5 0.3 fusion.24
  125.9 36.3 %reduce-scatter.5.cloned.1.call-done = bf16[72,4096]{1,0:T(8,128)(2,1)} async-done(((bf16[576,4096]{1,0:T(8,128)(2,1)}), bf16[72,4096]{1,0:T(8,128)(2,1)}) %reduce-scatter.5.cloned.1.call-update) | async-done | bytes 589840 | tf_op jit(solution)/shard_map/reduce_scatter | solution.py:110
  162.1 0.0 copy-done.1
  162.1 0.0 copy-done.4
  162.1 1.4 fusion.28
  163.6 0.0 copy-done
  163.6 2.6 fusion.37
  166.2 0.0 all-gather.4.cloned.1.call-update
  166.3 0.2 reduce-scatter.3.cloned.1.call-start
  166.5 50.0 %all-gather.4.cloned.1.call-done = bf16[576,4096]{1,0:T(8,128)(2,1)} async-done(((bf16[72,4096]{1,0:T(8,128)(2,1)}), bf16[576,4096]{1,0:T(8,128)(2,1)}) %all-gather.4.cloned.1.call-update) | async-done | bytes 4718608 | tf_op jit(solution)/shard_map/all_gather | solution.py:74
  216.5 11.5 %fusion.2 = f32[576,1536]{1,0:T(8,128)S(1)} fusion(bf16[576,4096]{1,0:T(8,128)(2,1)} %all-gather.4.cloned.1.call-done, bf16[1,1,4096,1536]{3,2,1,0:T(8,128)(2,1)} %param.20), kind=kOutput, calls=%fused_computation.2 | convolution fusion | flops 7247757312 | bytes 20840448 | tf_op jit(solution)/shard_map/dot_general | solution.py:76
  227.9 8.4 %multiply_convert_fusion = bf16[576,4096]{1,0:T(8,128)(2,1)} fusion(f32[576]{0:T(1024)S(1)} %get-tuple-element.5, bf16[1,1,768,4096]{3,2,1,0:T(8,128)(2,1)} %param.21, f32[576,1536]{1,0:T(8,128)S(1)} %fusion.2), kind=kOutput, calls=%fused_computation.6 | convolution fusion | flops 3631251456 | bytes 14551296 | tf_op jit(solution)/shard_map/dot_general | solution.py:80
  236.3 0.0 reduce-scatter.3.cloned.1.call-update
  236.3 53.9 %reduce-scatter.3.cloned.1.call-done = bf16[72,4096]{1,0:T(8,128)(2,1)} async-done(((bf16[576,4096]{1,0:T(8,128)(2,1)}), bf16[72,4096]{1,0:T(8,128)(2,1)}) %reduce-scatter.3.cloned.1.call-update) | async-done | bytes 589840 | tf_op jit(solution)/shard_map/reduce_scatter | solution.py:82
  290.3 2.0 fusion.36
  (10 shorter events, 0.1 us)
Async XLA Ops:
  7.2 20.0 %copy-start.5 = (f32[1,72,4]{1,2,0:T(4,128)S(1)}, f32[1,72,4]{1,2,0:T(4,128)}, u32[]{:S(2)}) copy-start(f32[1,72,4]{1,2,0:T(4,128)} %param.19) | copy-start | bytes 3460
  7.2 20.0 %copy-start.6 = (f32[1,72,4]{1,2,0:T(4,128)S(1)}, f32[1,72,4]{1,2,0:T(4,128)}, u32[]{:S(2)}) copy-start(f32[1,72,4]{1,2,0:T(4,128)} %param.17) | copy-start | bytes 3460
  7.2 20.1 %copy-start.7 = (s32[1,72,4]{1,2,0:T(4,128)S(1)}, s32[1,72,4]{1,2,0:T(4,128)}, u32[]{:S(2)}) copy-start(s32[1,72,4]{1,2,0:T(4,128)} %param.18) | copy-start | bytes 3460
  7.2 20.1 %copy-start.8 = (s32[1,72,4]{1,2,0:T(4,128)S(1)}, s32[1,72,4]{1,2,0:T(4,128)}, u32[]{:S(2)}) copy-start(s32[1,72,4]{1,2,0:T(4,128)} %param.16) | copy-start | bytes 3460
  7.2 50.1 %copy-start.2 = (bf16[1,1,360,1536]{3,2,1,0:T(8,128)(2,1)S(1)}, bf16[1,1,360,1536]{3,2,1,0:T(8,128)(2,1)}, u32[]{:S(2)}) copy-start(bf16[1,1,360,1536]{3,2,1,0:T(8,128)(2,1)} %param.14) | copy-start | bytes 3317764
  7.2 73.2 %all-gather.6.cloned.1.call-start = ((), (), s32[]{:S(2)}) async-start(), calls=%async_computation.5 | async-start | bytes 5308416 | tf_op jit(solution)/shard_map/all_gather | solution.py:75
  7.3 17.9 %collective-permute-start.8 = (bf16[1,72,4096]{2,1,0:T(8,128)(2,1)}, bf16[1,72,4096]{2,1,0:T(8,128)(2,1)S(1)}, u32[]{:S(2)}, u32[]{:S(2)}) collective-permute-start(bf16[1,72,4096]{2,1,0:T(8,128)(2,1)} %param.12), channel_id=1, source_target_pairs={{0,8},{8,16},{16,24},{1,9},{9,17},{17,25},{2,10},{10,18},{18,26},{... | collective-permute-start | bytes 1769480 | tf_op jit(solution)/shard_map/ppermute | solution.py:22
  27.1 135.0 %reduce-scatter.5.cloned.1.call-start = ((), (), s32[]{:S(2)}) async-start(), calls=%async_computation.4 | async-start | bytes 5308416 | tf_op jit(solution)/shard_map/reduce_scatter | solution.py:110
  27.3 4.9 %collective-permute-start.1 = (f32[72,16]{0,1:T(8,128)S(1)}, f32[72,16]{0,1:T(8,128)S(1)}, u32[]{:S(2)}, u32[]{:S(2)}) collective-permute-start(f32[72,16]{0,1:T(8,128)S(1)} %pad_maximum_fusion), channel_id=1, source_target_pairs={{0,1},{1,2},{2,3},{3,4},{4,5},{5,6},{6,7},{7,0},{8,9},{9,10},{10,1... | collective-permute-start | bytes 13832 | tf_op jit(solution)/shard_map/ppermute | solution.py:13
  32.2 4.9 %collective-permute-start.2 = (f32[72,16]{0,1:T(8,128)S(1)}, f32[72,16]{0,1:T(8,128)S(1)}, u32[]{:S(2)}, u32[]{:S(2)}) collective-permute-start(f32[72,16]{0,1:T(8,128)S(1)} %collective-permute-done.1), channel_id=1, source_target_pairs={{0,1},{1,2},{2,3},{3,4},{4,5},{5,6},{6,7},{7,0},{8,9},{9,10},{10,1... | collective-permute-start | bytes 13832 | tf_op jit(solution)/shard_map/ppermute | solution.py:13
  37.1 5.0 %collective-permute-start.3 = (f32[72,16]{0,1:T(8,128)S(1)}, f32[72,16]{0,1:T(8,128)S(1)}, u32[]{:S(2)}, u32[]{:S(2)}) collective-permute-start(f32[72,16]{0,1:T(8,128)S(1)} %collective-permute-done.2), channel_id=1, source_target_pairs={{0,1},{1,2},{2,3},{3,4},{4,5},{5,6},{6,7},{7,0},{8,9},{9,10},{10,1... | collective-permute-start | bytes 13832 | tf_op jit(solution)/shard_map/ppermute | solution.py:13
  42.1 5.0 %collective-permute-start.4 = (f32[72,16]{0,1:T(8,128)S(1)}, f32[72,16]{0,1:T(8,128)S(1)}, u32[]{:S(2)}, u32[]{:S(2)}) collective-permute-start(f32[72,16]{0,1:T(8,128)S(1)} %collective-permute-done.3), channel_id=1, source_target_pairs={{0,1},{1,2},{2,3},{3,4},{4,5},{5,6},{6,7},{7,0},{8,9},{9,10},{10,1... | collective-permute-start | bytes 13832 | tf_op jit(solution)/shard_map/ppermute | solution.py:13
  47.2 5.1 %collective-permute-start.5 = (f32[72,16]{0,1:T(8,128)S(1)}, f32[72,16]{0,1:T(8,128)S(1)}, u32[]{:S(2)}, u32[]{:S(2)}) collective-permute-start(f32[72,16]{0,1:T(8,128)S(1)} %collective-permute-done.4), channel_id=1, source_target_pairs={{0,1},{1,2},{2,3},{3,4},{4,5},{5,6},{6,7},{7,0},{8,9},{9,10},{10,1... | collective-permute-start | bytes 13832 | tf_op jit(solution)/shard_map/ppermute | solution.py:13
  52.2 5.1 %collective-permute-start.6 = (f32[72,16]{0,1:T(8,128)S(1)}, f32[72,16]{0,1:T(8,128)S(1)}, u32[]{:S(2)}, u32[]{:S(2)}) collective-permute-start(f32[72,16]{0,1:T(8,128)S(1)} %collective-permute-done.5), channel_id=1, source_target_pairs={{0,1},{1,2},{2,3},{3,4},{4,5},{5,6},{6,7},{7,0},{8,9},{9,10},{10,1... | collective-permute-start | bytes 13832 | tf_op jit(solution)/shard_map/ppermute | solution.py:13
  57.3 5.1 %collective-permute-start.7 = (f32[72,16]{0,1:T(8,128)S(1)}, f32[72,16]{0,1:T(8,128)S(1)}, u32[]{:S(2)}, u32[]{:S(2)}) collective-permute-start(f32[72,16]{0,1:T(8,128)S(1)} %collective-permute-done.6), channel_id=1, source_target_pairs={{0,1},{1,2},{2,3},{3,4},{4,5},{5,6},{6,7},{7,0},{8,9},{9,10},{10,1... | collective-permute-start | bytes 13832 | tf_op jit(solution)/shard_map/ppermute | solution.py:13
  108.2 1.1 copy-start.3
  108.2 53.9 %copy-start.1 = (bf16[1,72,4096]{2,1,0:T(8,128)(2,1)S(1)}, bf16[1,72,4096]{2,1,0:T(8,128)(2,1)}, u32[]{:S(2)}) copy-start(bf16[1,72,4096]{2,1,0:T(8,128)(2,1)} %param.13) | copy-start | bytes 1769476
  108.2 53.9 %copy-start.4 = (f32[1,4096]{1,0:T(1,128)S(1)}, f32[1,4096]{1,0:T(1,128)}, u32[]{:S(2)}) copy-start(f32[1,4096]{1,0:T(1,128)} %param.15) | copy-start | bytes 49156
  108.2 55.4 %copy-start = (bf16[1,72,4096]{2,1,0:T(8,128)(2,1)S(1)}, bf16[1,72,4096]{2,1,0:T(8,128)(2,1)}, u32[]{:S(2)}) copy-start(bf16[1,72,4096]{2,1,0:T(8,128)(2,1)} %broadcast_select_fusion) | copy-start | bytes 1769476
  108.2 108.2 %all-gather.4.cloned.1.call-start = ((), (), s32[]{:S(2)}) async-start(), calls=%async_computation.2 | async-start | bytes 5308416 | tf_op jit(solution)/shard_map/all_gather | solution.py:74
  109.2 16.3 %collective-permute-start = (bf16[1,72,4096]{2,1,0:T(8,128)(2,1)S(1)}, bf16[1,72,4096]{2,1,0:T(8,128)(2,1)S(1)}, u32[]{:S(2)}, u32[]{:S(2)}) collective-permute-start(bf16[1,72,4096]{2,1,0:T(8,128)(2,1)S(1)} %copy-done.3), channel_id=1, source_target_pairs={{0,8},{8,16},{16,24},{1,9},{9,17},{17,25},{2,10},{10,18},{18,26},{... | collective-permute-start | bytes 1769480 | tf_op jit(solution)/shard_map/ppermute | solution.py:22
  166.3 124.0 %reduce-scatter.3.cloned.1.call-start = ((), (), s32[]{:S(2)}) async-start(), calls=%async_computation.3 | async-start | bytes 5308416 | tf_op jit(solution)/shard_map/reduce_scatter | solution.py:82
Sparse Core Ops, SparseCore 0:
  27.2 53.1 all-gather.5
  108.3 53.7 reduce-scatter.4
  166.4 50.0 all-gather.3
  236.5 53.7 reduce-scatter.2
